TPU v7x, 128 devices: a whole 4x4x4 slice. The times are simulated.
128 devices in a mesh: grp: 16 (over x, z_hi, core), seq: 8 (over y, z_lo).
Axes of the slice: x: 4, y: 4, z: 4 (z_hi: 2, z_lo: 2; z = z_hi * 2 + z_lo), core: 2. Of those that a mesh axis runs over, the one named last changes fastest.
Arguments:
- lengths: int32 [32], replicated, may hold values from 64 to 2048, as said below
- group_of: int32 [32], replicated, may hold values from 0 to 15, as said below
- query_pre: bfloat16 [32768, 8192], P(('grp', 'seq')), may hold values from -170 to 170
- key_pre: bfloat16 [32768, 1024], P(('grp', 'seq')), may hold values from -7 to 7
- value_pre: bfloat16 [32768, 1024], P(('grp', 'seq')), may hold values from -4 to 4
- query_new: bfloat16 [32, 8192], P(None, 'seq'), may hold values from -170 to 170
- key_new: bfloat16 [32, 1024], P(None, 'seq'), may hold values from -4 to 4
- value_new: bfloat16 [32, 1024], P(None, 'seq'), may hold values from -4 to 4
- hidden_new: bfloat16 [32, 8192], P(None, 'grp'), may hold values from -3 to 3
- out_weight: bfloat16 [8192, 8192], P('seq', 'grp'), may hold values from -0.0625 to 0.0625
- norm_gain: bfloat16 [8192], P('grp'), may hold values from 0.099609375 to 1.8984375
- gate_weight: bfloat16 [8192, 16384], P('grp', 'seq'), may hold values from -0.0625 to 0.0625
- up_weight: bfloat16 [8192, 16384], P('grp', 'seq'), may hold values from -0.0625 to 0.0625
- down_weight: bfloat16 [16384, 8192], P('seq', 'grp'), may hold values from -0.046875 to 0.046875
Outputs:
- prefill_attention: bfloat16 [32768, 8192], P(('grp', 'seq'))
- decode_hidden: bfloat16 [32, 8192], P(None, ('grp', 'seq'))
Inputs may be any that keep to these rules, and one draw needn't show every extreme that they name: Two requests have length exactly 2048 and are alone in their groups; the others have lengths from 64 to 512; the lengths in one group sum to at most 2048. `group_of`: every group holds at least one request and at most three.
All inputs are finite; a program needn't handle non-finite values.
Results may differ from a plain program's by a relative error of at most 0.0095.
Values may be sent and summed in bfloat16 or wider, within the bound.
A program may use at most 320 MiB of HBM per device.

v0:
```python
import math
import jax
import jax.numpy as jnp
from jax import lax
from jax.sharding import PartitionSpec as P

D = 8192
H = 64
KVH = 8
HD = 128
NEGATIVE = -1e30


def request_starts(lengths, group_of):
    index = jnp.arange(lengths.shape[0], dtype=jnp.int32)
    same = group_of[None, :] == group_of[:, None]
    before = index[None, :] < index[:, None]
    return jnp.sum(jnp.where(same & before, lengths[None, :], 0), axis=1)


def slot_owner(group_idx, starts, lengths, group_of, count):
    slots = jnp.arange(count, dtype=jnp.int32)
    inside = (
        (group_of[None, :] == group_idx)
        & (slots[:, None] >= starts[None, :])
        & (slots[:, None] < (starts + lengths)[None, :])
    )
    labels = jnp.arange(lengths.shape[0], dtype=jnp.int32) + 1
    return jnp.sum(jnp.where(inside, labels[None, :], 0), axis=1) - 1


def block_scores(queries, keys, owner_rows, owner_cols, row_first):
    count_q = queries.shape[0]
    count_k = keys.shape[0]
    kv_heads = keys.shape[1] // HD
    grouped = queries.shape[1] // (HD * kv_heads)
    query_heads = queries.reshape(count_q, kv_heads, grouped, HD)
    key_heads = keys.reshape(count_k, kv_heads, HD)
    scores = jnp.einsum(
        "qkgd,tkd->kgqt", query_heads, key_heads, preferred_element_type=jnp.float32
    ) * (1.0 / math.sqrt(HD))
    rows = row_first + jnp.arange(count_q, dtype=jnp.int32)
    columns = jnp.arange(count_k, dtype=jnp.int32)
    allowed = (
        (owner_rows[:, None] == owner_cols[None, :])
        & (owner_rows[:, None] >= 0)
        & (columns[None, :] <= rows[:, None])
    )
    return (jnp.where(allowed[None, None], scores, NEGATIVE), allowed)


def online_step(carry, queries, keys, values, owner_rows, owner_cols, row_first):
    top, total, accum = carry
    count = keys.shape[0]
    kv_heads = keys.shape[1] // HD
    scores, allowed = block_scores(queries, keys, owner_rows, owner_cols, row_first)
    new_top = jnp.maximum(top, jnp.max(scores, axis=-1))
    weights = jnp.where(allowed[None, None], jnp.exp(scores - new_top[..., None]), 0.0)
    total = jnp.sum(weights, axis=-1)
    value_heads = values.reshape(count, kv_heads, HD)
    mixed = jnp.einsum(
        "kgqt,tkd->qkgd",
        weights.astype(jnp.bfloat16),
        value_heads,
        preferred_element_type=jnp.float32,
    )
    accum = mixed
    return (new_top, total, accum)


def empty_carry(rows, kv_heads, grouped):
    init_top = jnp.full((kv_heads, grouped, rows), NEGATIVE, jnp.float32)
    init_total = jnp.zeros((kv_heads, grouped, rows), jnp.float32)
    init_acc = jnp.zeros((rows, kv_heads, grouped, HD), jnp.float32)
    return (init_top, init_total, init_acc)


def finish(mixed, total, owner_rows):
    live = owner_rows >= 0
    denom = jnp.where(live[None, None, :], total, 1.0)
    result = mixed / jnp.transpose(denom, (2, 0, 1))[..., None]
    result = jnp.where(live[:, None, None, None], result, 0.0)
    return result.reshape(result.shape[0], -1).astype(jnp.bfloat16)


def decode_attend(query_new, key_new, value_new, cache_keys, cache_values, owners):
    requests = query_new.shape[0]
    kv_heads = cache_keys.shape[1] // HD
    grouped = query_new.shape[1] // (HD * kv_heads)
    query_heads = query_new.reshape(requests, kv_heads, grouped, HD)
    key_heads = cache_keys.reshape(cache_keys.shape[0], kv_heads, HD)
    value_heads = cache_values.reshape(cache_values.shape[0], kv_heads, HD)
    scale = 1.0 / math.sqrt(HD)
    scores = (
        jnp.einsum("rkgd,tkd->rkgt", query_heads, key_heads, preferred_element_type=jnp.float32)
        * scale
    )
    own = (
        jnp.einsum(
            "rkgd,rkd->rkg",
            query_heads,
            key_new.reshape(requests, kv_heads, HD),
            preferred_element_type=jnp.float32,
        )
        * scale
    )
    match = owners[None, :] == jnp.arange(requests, dtype=jnp.int32)[:, None]
    scores = jnp.where(match[:, None, None, :], scores, NEGATIVE)
    top = jnp.maximum(jnp.max(scores, axis=-1), own)
    weights = jnp.where(match[:, None, None, :], jnp.exp(scores - top[..., None]), 0.0)
    own_weight = jnp.exp(own - top)
    total = jnp.sum(weights, axis=-1) + own_weight
    mixed = jnp.einsum(
        "rkgt,tkd->rkgd",
        weights.astype(jnp.bfloat16),
        value_heads,
        preferred_element_type=jnp.float32,
    )
    own_value = value_new.reshape(requests, kv_heads, 1, HD).astype(jnp.float32)
    mixed = mixed + own_weight.astype(jnp.bfloat16).astype(jnp.float32)[..., None] * own_value
    return (mixed / total[..., None]).reshape(requests, -1).astype(jnp.bfloat16)


def shards(
    lengths,
    group_of,
    query_pre,
    key_pre,
    value_pre,
    query_new,
    key_new,
    value_new,
    hidden_new,
    out_weight,
    norm_gain,
    gate_weight,
    up_weight,
    down_weight,
):
    seq_count = lax.axis_size("seq")
    seq_index = lax.axis_index("seq")
    group_idx = lax.axis_index("grp")
    tokens_dev = query_pre.shape[0]
    group_slots = tokens_dev * seq_count
    starts = request_starts(lengths, group_of)
    owners = slot_owner(group_idx, starts, lengths, group_of, group_slots)
    cache_keys, cache_values = (
        lax.all_to_all(key_pre, "seq", split_axis=1, concat_axis=0, tiled=True),
        lax.all_to_all(value_pre, "seq", split_axis=1, concat_axis=0, tiled=True),
    )
    my_first = seq_index * tokens_dev
    my_last = my_first + tokens_dev - 1
    owner_rows = lax.dynamic_slice_in_dim(owners, my_first, tokens_dev, 0)
    any_live = jnp.any(owner_rows >= 0)
    grouped = H // KVH
    piece_keys = lax.all_gather(key_pre, "seq", axis=0, tiled=True)
    piece_values = lax.all_gather(value_pre, "seq", axis=0, tiled=True)
    needed = (jnp.int32(0) <= my_last) & any_live

    def attend(state):
        return online_step(state, query_pre, piece_keys, piece_values, owner_rows, owners, my_first)

    def keep(state):
        return state

    top, total, accum = lax.cond(needed, attend, keep, empty_carry(tokens_dev, KVH, grouped))
    prefill_attention = finish(accum, total, owner_rows)
    attended = decode_attend(query_new, key_new, value_new, cache_keys, cache_values, owners)
    mine = group_of == group_idx
    attended = jnp.where(mine[:, None], attended, jnp.zeros_like(attended))
    decode_att = lax.psum(attended, "grp").astype(jnp.float32).astype(jnp.bfloat16)
    proj_part = jnp.dot(decode_att, out_weight, preferred_element_type=jnp.float32)
    projected = lax.psum(proj_part, "seq")
    resid = hidden_new.astype(jnp.float32) + projected
    squares = lax.psum(jnp.sum(resid * resid, axis=-1), "grp")
    normed = (
        resid * lax.rsqrt(squares / D + 1e-05)[:, None] * norm_gain.astype(jnp.float32)[None, :]
    ).astype(jnp.bfloat16)
    gate_part = jnp.dot(normed, gate_weight, preferred_element_type=jnp.float32)
    upper_part = jnp.dot(normed, up_weight, preferred_element_type=jnp.float32)
    gate, upper = lax.psum((gate_part, upper_part), "grp")
    hidden = (jax.nn.silu(gate) * upper).astype(jnp.bfloat16)
    down_part = jnp.dot(hidden, down_weight, preferred_element_type=jnp.float32)
    down_share = lax.psum_scatter(down_part, "seq", scatter_dimension=1, tiled=True)
    width = down_share.shape[1]
    resid_share = lax.dynamic_slice_in_dim(resid, seq_index * width, width, 1)
    decode_hidden = (resid_share + down_share).astype(jnp.bfloat16)
    return (prefill_attention, decode_hidden)


def solution(mesh):
    return jax.shard_map(
        shards,
        mesh=mesh,
        in_specs=(
            P(),
            P(),
            P(("grp", "seq"), None),
            P(("grp", "seq"), None),
            P(("grp", "seq"), None),
            P(None, "seq"),
            P(None, "seq"),
            P(None, "seq"),
            P(None, "grp"),
            P("seq", "grp"),
            P("grp"),
            P("grp", "seq"),
            P("grp", "seq"),
            P("seq", "grp"),
        ),
        out_specs=(P(("grp", "seq"), None), P(None, ("grp", "seq"))),
        check_vma=False,
    )
```

profile of v0, /device:TPU:23, one launch (start us, length us, event | category | flops | bytes accessed | tf_op | source)
XLA Modules:
  0.0 828.9 jit_solution(12726307764702582196)
XLA Ops:
  7.2 2.1 copy_bitcast_fusion.2
  9.3 5.6 all-to-all-start
  15.5 0.9 select_reduce_fusion.1
  17.1 0.8 copy.74
  18.0 1.9 copy_bitcast_fusion.1
  21.8 5.5 all-to-all-start.1
  27.9 1.3 copy-done.1
  29.7 3.8 all-to-all-done.1
  33.5 2.1 fusion.25
  36.4 124.9 %all-reduce.5.cloned.1.call-done = bf16[32,1024]{1,0:T(8,128)(2,1)} async-done(((bf16[32,1024]{1,0:T(8,128)(2,1)}), bf16[32,1024]{1,0:T(8,128)(2,1)}) %all-reduce.5.cloned.1.call-update) | async-done | bytes 65552 | tf_op jit(solution)/shard_map/psum | solution.py:171
  161.3 2.2 fusion.47
  163.6 70.2 %all-reduce.7.cloned.1.call-done = f32[32,512]{1,0:T(8,128)} async-done(((f32[32,512]{1,0:T(8,128)}), f32[32,512]{1,0:T(8,128)}) %all-reduce.7.cloned.1.call-update) | async-done | bytes 65552 | tf_op jit(solution)/shard_map/psum | solution.py:173
  233.7 1.0 multiply_reduce_fusion
  234.7 33.4 %psum.37 = f32[32]{0:T(128)S(1)} all-reduce(f32[32]{0:T(128)S(1)} %get-tuple-element.28), channel_id=1, replica_groups=mesh['grp'=16,'seq'=8] {'grp'}, use_global_device_ids=true, to_apply=%region_12.13 | all-reduce | flops 32 | bytes 256 | tf_op jit(solution)/shard_map/psum | solution.py:175
  268.1 1.2 fusion.44
  269.3 2.8 fusion.43
  272.2 139.1 %all-reduce.9.cloned.1.call-done = (f32[32,2048]{1,0:T(8,128)}, f32[32,2048]{1,0:T(8,128)}) async-done(((f32[32,2048]{1,0:T(8,128)}, f32[32,2048]{1,0:T(8,128)}), (f32[32,2048]{1,0:T(8,128)}, f32[32,2048]{1,0:T(8,128)})) %all-reduce.9.cloned.1.call-update) | async-done | bytes 524304 | tf_op jit(solution)/shard_map/psum | solution.py:181
  411.3 3.4 convolution_bitcast_fusion
  415.9 1.2 fusion.45
  417.8 28.3 %reduce-scatter.4.cloned.1.call-done = f32[64,32]{1,0:T(8,128)} async-done(((f32[512,32]{1,0:T(8,128)}), f32[64,32]{1,0:T(8,128)}) %reduce-scatter.4.cloned.1.call-update) | async-done | bytes 8208
  447.6 98.0 %all-gather.3.cloned.1.call-done = bf16[2048,1024]{1,0:T(8,128)(2,1)} async-done(((bf16[256,1024]{1,0:T(8,128)(2,1)}), bf16[2048,1024]{1,0:T(8,128)(2,1)}) %all-gather.3.cloned.1.call-update) | async-done | bytes 4194320 | tf_op jit(solution)/shard_map/all_gather | solution.py:156
  545.6 93.8 %all-gather.5.cloned.1.call-done = bf16[2048,1024]{1,0:T(8,128)(2,1)} async-done(((bf16[256,1024]{1,0:T(8,128)(2,1)}), bf16[2048,1024]{1,0:T(8,128)(2,1)}) %all-gather.5.cloned.1.call-update) | async-done | bytes 4194320 | tf_op jit(solution)/shard_map/all_gather | solution.py:157
  639.4 163.5 %conditional.1 = (f32[8,8,256]{2,1,0:T(8,128)}, f32[256,8,8,128]{3,0,2,1:T(8,128)}) conditional(s32[]{:T(128)} %convert_element_type.50, () %tuple.16, (s32[256]{0:T(256)S(1)}, s32[2048]{0:T(1024)S(1)}, s32[]{:T(128)}, bf16[2048,1024]{1,0:T(8,128)(2,1)}, bf16[256,8192]{1,0:T(8,128)(2,1)}, /*index=5*/bf16[2048,1024]{1,0:T(8,128)(2,1)}) %tuple.17), branch_computations={%region_3.4_spmd, %region_4.7_spmd} | conditional | flops 17618157568 | bytes 468070976 | solution.py:166
  640.2 5.4 copy.67
  645.6 3.2 copy.68
  648.8 52.7 %fusion = (f32[8,8,256]{2,1,0:T(8,128)S(1)}, f32[8,2048,256,8]{2,1,3,0:T(8,128)}) fusion(pred[256,2048]{0,1:T(8,128)(4,1)S(1)} %fusion.15, bf16[256,8,8,128]{3,2,1,0:T(8,128)(2,1)} %bitcast.116, bf16[2048,8,128,1]{2,1,0,3:T(8,128)(2,1)} %bitcast.117), kind=kOutput, calls=%fused_computation.2 | convolution fusion | flops 8690581504 | bytes 143196160 | tf_op jit(solution)/shard_map/cond/branch_1_fun/qkgd,tkd->kgqt/dot_general | solution.py:39
  701.5 5.3 copy.69
  706.8 54.3 %fusion.10 = f32[256,8,8,128]{3,0,2,1:T(8,128)} fusion(bf16[2048,8,128,1]{2,1,0,3:T(8,128)(2,1)} %bitcast.123, f32[8,2048,256,8]{2,1,3,0:T(8,128)} %get-tuple-element.34, f32[8,8,256]{2,1,0:T(8,128)S(1)} %broadcast_maximum_fusion, pred[256,2048]{0,1:T(8,128)(4,1)S(1)} %fusion.15), kind=kOutput, calls=%fused_computation.11 | convolution fusion | flops 8757706752 | bytes 147390464 | tf_op jit(solution)/shard_map/cond/branch_1_fun/kgqt,tkd->qkgd/dot_general | solution.py:61
  761.1 41.9 %fusion.2 = f32[8,8,256]{2,1,0:T(8,128)} fusion(f32[8,2048,256,8]{2,1,3,0:T(8,128)} %get-tuple-element.34, f32[8,8,256]{2,1,0:T(8,128)S(1)} %broadcast_maximum_fusion, pred[256,2048]{0,1:T(8,128)(4,1)S(1)} %fusion.15), kind=kLoop, calls=%fused_computation.4 | loop fusion | flops 167755776 | bytes 134873088 | tf_op jit(solution)/shard_map/cond/branch_1_fun/reduce_sum | solution.py:59
  803.8 5.4 select_convert_fusion
  809.2 2.7 copy.51
  811.9 10.2 %copy.100 = bf16[32,8,64,128]{3,1,2,0:T(8,128)(2,1)} copy(bf16[32,8,64,128]{3,2,1,0:T(8,128)(2,1)S(1)} %bitcast.118) | data formatting | bytes 8388608
  (50 shorter events, 9.4 us)
Async XLA Ops:
  7.2 261.0 %copy-start = (bf16[512,2048]{1,0:T(8,128)(2,1)S(1)}, bf16[512,2048]{1,0:T(8,128)(2,1)}, u32[]{:S(2)}) copy-start(bf16[512,2048]{1,0:T(8,128)(2,1)} %param.27) | copy-start | bytes 6291460
  7.2 20.1 %copy-start.3 = (bf16[32,1024]{1,0:T(8,128)(2,1)S(1)}, bf16[32,1024]{1,0:T(8,128)(2,1)}, u32[]{:S(2)}) copy-start(bf16[32,1024]{1,0:T(8,128)(2,1)} %param.21) | copy-start | bytes 196612
  9.3 12.5 %all-to-all-start = ((bf16[256,8,128]{2,0,1:T(8,128)(2,1)}), bf16[256,8,128]{2,0,1:T(8,128)(2,1)S(1)}, u32[]{:S(2)}, u32[]{:S(2)}) async-start(bf16[256,8,128]{2,0,1:T(8,128)(2,1)} %copy_bitcast_fusion.2), calls=%async_computation | async-start | bytes 1048576 | tf_op jit(solution)/shard_map/all_to_all | solution.py:148
  21.8 11.7 %all-to-all-start.1 = ((bf16[256,8,128]{2,0,1:T(8,128)(2,1)}), bf16[256,8,128]{2,0,1:T(8,128)(2,1)S(1)}, u32[]{:S(2)}, u32[]{:S(2)}) async-start(bf16[256,8,128]{2,0,1:T(8,128)(2,1)} %copy_bitcast_fusion.1), calls=%async_computation.1 | async-start | bytes 1048576 | tf_op jit(solution)/shard_map/all_to_all | solution.py:149
  27.3 134.0 %all-reduce.5.cloned.1.call-start = ((), (), s32[]{:S(2)}) async-start(), calls=%async_computation.5 | async-start | bytes 131072 | tf_op jit(solution)/shard_map/psum | solution.py:171
  27.8 1.3 copy-start.1
  27.9 135.7 %copy-start.6 = (bf16[512]{0:T(512)(128)(2,1)S(1)}, bf16[512]{0:T(512)(128)(2,1)}, u32[]{:S(2)}) copy-start(bf16[512]{0:T(512)(128)(2,1)} %param.26) | copy-start | bytes 3076
  27.9 205.9 %copy-start.4 = (bf16[32,512]{1,0:T(8,128)(2,1)S(1)}, bf16[32,512]{1,0:T(8,128)(2,1)}, u32[]{:S(2)}) copy-start(bf16[32,512]{1,0:T(8,128)(2,1)} %param.24) | copy-start | bytes 98308
  36.4 197.4 %all-reduce.7.cloned.1.call-start = ((), (), s32[]{:S(2)}) async-start(), calls=%async_computation.6 | async-start | bytes 131072 | tf_op jit(solution)/shard_map/psum | solution.py:173
  163.5 247.8 %all-reduce.9.cloned.1.call-start = ((), (), s32[]{:S(2)}) async-start(), calls=%async_computation.8 | async-start | bytes 1048576 | tf_op jit(solution)/shard_map/psum | solution.py:181
  272.2 173.9 %reduce-scatter.4.cloned.1.call-start = ((), (), s32[]{:S(2)}) async-start(), calls=%async_computation.7 | async-start | bytes 294912
  414.8 130.9 %all-gather.3.cloned.1.call-start = ((), (), s32[]{:S(2)}) async-start(), calls=%async_computation.3 | async-start | bytes 4718592 | tf_op jit(solution)/shard_map/all_gather | solution.py:156
  415.4 224.1 %all-gather.5.cloned.1.call-start = ((), (), s32[]{:S(2)}) async-start(), calls=%async_computation.4 | async-start | bytes 4718592 | tf_op jit(solution)/shard_map/all_gather | solution.py:157
  639.4 163.5 %copy-start.5 = (pred[256]{0:T(512)(128)(4,1)S(1)}, pred[256]{0:T(512)(128)(4,1)}, u32[]{:S(2)}) copy-start(pred[256]{0:T(512)(128)(4,1)} %get-tuple-element.31) | copy-start | bytes 772
  640.2 5.4 copy-start.2
Sparse Core Ops, SparseCore 0:
  36.5 124.7 all-reduce.4
  164.5 69.2 all-reduce.6
  272.3 138.9 all-reduce.8
  414.9 31.1 reduce-scatter.3
  447.6 98.0 all-gather.2
  547.1 92.2 all-gather.4
where the time goes:
time: 830 us; the launch traced here: 829 us
  waiting for transfers between devices  559 us (67%)
  matrix products  120 us (14%)
  other arithmetic  56.1 us (7%)
  local copies, waits for them, and re-layouts  33.9 us (4%)
  blocking collectives  33.4 us (4%)
  between operations  14.9 us (2%)
  starting transfers between devices  11.3 us (1%)
    psum x1, waiting for transfers between devices, shards(): gate, upper = lax.psum((gate_part, upper_part), 'grp')  139 us
    psum x1, waiting for transfers between devices, shards(): lax.psum(attended, 'grp').astype(jnp.float32).astype(jnp.bfloat16)  125 us
    all_gather x1, waiting for transfers between devices, shards(): piece_keys = lax.all_gather(key_pre, 'seq', axis=0, tiled=True)  98 us
    all_gather x1, waiting for transfers between devices, shards(): piece_values = lax.all_gather(value_pre, 'seq', axis=0, tiled=True)  93.8 us
    psum x1, waiting for transfers between devices, shards(): projected = lax.psum(proj_part, 'seq')  70.2 us
    dot_general x1, matrix products, online_step(): jnp.einsum('kgqt,tkd->qkgd', weights.astype(jnp.bfloat16), value_heads, p...  54.3 us
    dot_general x1, matrix products, block_scores(): jnp.einsum('qkgd,tkd->kgqt', query_heads, key_heads, preferred_element_ty...  52.7 us
    reduce_sum x1, other arithmetic, online_step(): total = jnp.sum(weights, axis=-1)  41.9 us
  transfers between devices with their start and end apart: 8, of which 7 were waited for; matrix products, arithmetic and copies ran while one was open for 1% of the time, Pallas kernels for 0%

commit v1 on v0

--- a/solution.py
+++ b/solution.py
@@ -154,7 +154,8 @@
     any_live = jnp.any(owner_rows >= 0)
     grouped = H // KVH
     piece_keys = lax.all_gather(key_pre, "seq", axis=0, tiled=True)
-    piece_values = lax.all_gather(value_pre, "seq", axis=0, tiled=True)
+    sent = jnp.stack([value_pre] * lax.axis_size("seq"))
+    piece_values = jnp.concatenate(lax.all_to_all(sent, "seq", 0, 0), axis=0)
     needed = (jnp.int32(0) <= my_last) & any_live
 
     def attend(state):

time: 830 us -> 776 us (0.935)
  waiting for transfers between devices: 559 us -> 498 us
    all_gather x1 -> x0, waiting for transfers between devices: 93.8 us -> none  [shards(): piece_values = lax.all_gather(value_pre, 'seq', axis=0, tiled=True)]
    unnamed x7 -> x6, waiting for transfers between devices: 29.4 us -> 58.9 us
  transfers between devices with their start and end apart: 8 -> 8, of which waited for: 7 -> 6; matrix products, arithmetic and copies ran while one was open for 1% -> 2% of each run, Pallas kernels for 0% -> 0%
where the time goes in v1:
time: 776 us; the launch traced here: 774 us
  waiting for transfers between devices  498 us (64%)
  matrix products  120 us (15%)
  other arithmetic  56.1 us (7%)
  local copies, waits for them, and re-layouts  36.4 us (5%)
  blocking collectives  33.4 us (4%)
  starting transfers between devices  16 us (2%)
  between operations  14.6 us (2%)
    psum x1, waiting for transfers between devices, shards(): gate, upper = lax.psum((gate_part, upper_part), 'grp')  139 us
    psum x1, waiting for transfers between devices, shards(): lax.psum(attended, 'grp').astype(jnp.float32).astype(jnp.bfloat16)  125 us
    all_gather x1, waiting for transfers between devices, shards(): piece_keys = lax.all_gather(key_pre, 'seq', axis=0, tiled=True)  101 us
    psum x1, waiting for transfers between devices, shards(): projected = lax.psum(proj_part, 'seq')  70.2 us
    unnamed x6, waiting for transfers between devices  58.9 us
    dot_general x1, matrix products, online_step(): jnp.einsum('kgqt,tkd->qkgd', weights.astype(jnp.bfloat16), value_heads, p...  54.3 us
    dot_general x1, matrix products, block_scores(): jnp.einsum('qkgd,tkd->kgqt', query_heads, key_heads, preferred_element_ty...  52.7 us
    reduce_sum x1, other arithmetic, online_step(): total = jnp.sum(weights, axis=-1)  41.9 us
  transfers between devices with their start and end apart: 8, of which 6 were waited for; matrix products, arithmetic and copies ran while one was open for 2% of the time, Pallas kernels for 0%

profile of v1, /device:TPU:23, one launch (start us, length us, event | category | flops | bytes accessed | tf_op | source)
XLA Modules:
  0.0 774.3 jit_solution(4400843240223652202)
XLA Ops:
  7.2 2.1 copy_bitcast_fusion.2
  9.3 5.6 all-to-all-start.1
  15.5 0.9 select_reduce_fusion.1
  18.0 1.9 copy_bitcast_fusion.1
  21.8 5.5 all-to-all-start.2
  27.9 1.3 copy-done.1
  29.7 3.8 all-to-all-done.2
  33.5 2.1 fusion.25
  36.4 124.9 %all-reduce.5.cloned.1.call-done = bf16[32,1024]{1,0:T(8,128)(2,1)} async-done(((bf16[32,1024]{1,0:T(8,128)(2,1)}), bf16[32,1024]{1,0:T(8,128)(2,1)}) %all-reduce.5.cloned.1.call-update) | async-done | bytes 65552 | tf_op jit(solution)/shard_map/psum | solution.py:172
  161.3 2.2 fusion.47
  163.6 70.2 %all-reduce.7.cloned.1.call-done = f32[32,512]{1,0:T(8,128)} async-done(((f32[32,512]{1,0:T(8,128)}), f32[32,512]{1,0:T(8,128)}) %all-reduce.7.cloned.1.call-update) | async-done | bytes 65552 | tf_op jit(solution)/shard_map/psum | solution.py:174
  233.7 1.0 multiply_reduce_fusion
  234.7 33.4 %psum.37 = f32[32]{0:T(128)S(1)} all-reduce(f32[32]{0:T(128)S(1)} %get-tuple-element.28), channel_id=1, replica_groups=mesh['grp'=16,'seq'=8] {'grp'}, use_global_device_ids=true, to_apply=%region_12.13 | all-reduce | flops 32 | bytes 256 | tf_op jit(solution)/shard_map/psum | solution.py:176
  268.1 1.2 fusion.44
  269.3 2.8 fusion.43
  272.2 139.1 %all-reduce.9.cloned.1.call-done = (f32[32,2048]{1,0:T(8,128)}, f32[32,2048]{1,0:T(8,128)}) async-done(((f32[32,2048]{1,0:T(8,128)}, f32[32,2048]{1,0:T(8,128)}), (f32[32,2048]{1,0:T(8,128)}, f32[32,2048]{1,0:T(8,128)})) %all-reduce.9.cloned.1.call-update) | async-done | bytes 524304 | tf_op jit(solution)/shard_map/psum | solution.py:182
  411.3 3.4 convolution_bitcast_fusion
  415.3 2.6 stack.2
  417.9 4.7 all-to-all-start
  422.6 1.2 fusion.45
  424.5 58.3 %reduce-scatter.4.cloned.1.call-done = f32[64,32]{1,0:T(8,128)} async-done(((f32[512,32]{1,0:T(8,128)}), f32[64,32]{1,0:T(8,128)}) %reduce-scatter.4.cloned.1.call-update) | async-done | bytes 8208
  484.3 100.9 %all-gather.2.cloned.1.call-done = bf16[2048,1024]{1,0:T(8,128)(2,1)} async-done(((bf16[256,1024]{1,0:T(8,128)(2,1)}), bf16[2048,1024]{1,0:T(8,128)(2,1)}) %all-gather.2.cloned.1.call-update) | async-done | bytes 4194320 | tf_op jit(solution)/shard_map/all_gather | solution.py:156
  585.2 163.5 %conditional.1 = (f32[8,8,256]{2,1,0:T(8,128)}, f32[256,8,8,128]{3,0,2,1:T(8,128)}) conditional(s32[]{:T(128)} %convert_element_type.50, () %tuple.16, (s32[256]{0:T(256)S(1)}, s32[2048]{0:T(1024)S(1)}, s32[]{:T(128)}, bf16[2048,1024]{1,0:T(8,128)(2,1)}, bf16[256,8192]{1,0:T(8,128)(2,1)}, /*index=5*/bf16[8,256,1024]{2,1,0:T(8,128)(2,1)}) %tuple.17), branch_computations={%region_3.4_spmd, %region_4.7_spmd} | conditional | flops 17618157568 | bytes 468070976 | solution.py:167
  585.9 5.4 copy.67
  591.3 3.2 copy.68
  594.5 52.7 %fusion = (f32[8,8,256]{2,1,0:T(8,128)S(1)}, f32[8,2048,256,8]{2,1,3,0:T(8,128)}) fusion(pred[256,2048]{0,1:T(8,128)(4,1)S(1)} %fusion.15, bf16[256,8,8,128]{3,2,1,0:T(8,128)(2,1)} %bitcast.117, bf16[2048,8,128,1]{2,1,0,3:T(8,128)(2,1)} %bitcast.118), kind=kOutput, calls=%fused_computation.2 | convolution fusion | flops 8690581504 | bytes 143196160 | tf_op jit(solution)/shard_map/cond/branch_1_fun/qkgd,tkd->kgqt/dot_general | solution.py:39
  647.2 5.3 copy.69
  652.5 54.3 %fusion.10 = f32[256,8,8,128]{3,0,2,1:T(8,128)} fusion(bf16[2048,8,128,1]{2,1,0,3:T(8,128)(2,1)} %bitcast.123, f32[8,2048,256,8]{2,1,3,0:T(8,128)} %get-tuple-element.34, f32[8,8,256]{2,1,0:T(8,128)S(1)} %broadcast_maximum_fusion, pred[256,2048]{0,1:T(8,128)(4,1)S(1)} %fusion.15), kind=kOutput, calls=%fused_computation.11 | convolution fusion | flops 8757706752 | bytes 147390464 | tf_op jit(solution)/shard_map/cond/branch_1_fun/kgqt,tkd->qkgd/dot_general | solution.py:61
  706.8 41.9 %fusion.2 = f32[8,8,256]{2,1,0:T(8,128)} fusion(f32[8,2048,256,8]{2,1,3,0:T(8,128)} %get-tuple-element.34, f32[8,8,256]{2,1,0:T(8,128)S(1)} %broadcast_maximum_fusion, pred[256,2048]{0,1:T(8,128)(4,1)S(1)} %fusion.15), kind=kLoop, calls=%fused_computation.4 | loop fusion | flops 167755776 | bytes 134873088 | tf_op jit(solution)/shard_map/cond/branch_1_fun/reduce_sum | solution.py:59
  749.5 5.4 select_convert_fusion
  754.9 2.7 copy.51
  757.6 10.2 %copy.100 = bf16[32,8,64,128]{3,1,2,0:T(8,128)(2,1)} copy(bf16[32,8,64,128]{3,2,1,0:T(8,128)(2,1)S(1)} %bitcast.119) | data formatting | bytes 8388608
  (52 shorter events, 9.7 us)
Async XLA Ops:
  7.2 261.0 %copy-start = (bf16[512,2048]{1,0:T(8,128)(2,1)S(1)}, bf16[512,2048]{1,0:T(8,128)(2,1)}, u32[]{:S(2)}) copy-start(bf16[512,2048]{1,0:T(8,128)(2,1)} %param.27) | copy-start | bytes 6291460
  7.2 20.1 %copy-start.4 = (bf16[32,1024]{1,0:T(8,128)(2,1)S(1)}, bf16[32,1024]{1,0:T(8,128)(2,1)}, u32[]{:S(2)}) copy-start(bf16[32,1024]{1,0:T(8,128)(2,1)} %param.21) | copy-start | bytes 196612
  9.3 12.5 %all-to-all-start.1 = ((bf16[256,8,128]{2,0,1:T(8,128)(2,1)}), bf16[256,8,128]{2,0,1:T(8,128)(2,1)S(1)}, u32[]{:S(2)}, u32[]{:S(2)}) async-start(bf16[256,8,128]{2,0,1:T(8,128)(2,1)} %copy_bitcast_fusion.2), calls=%async_computation.1 | async-start | bytes 1048576 | tf_op jit(solution)/shard_map/all_to_all | solution.py:148
  21.8 11.7 %all-to-all-start.2 = ((bf16[256,8,128]{2,0,1:T(8,128)(2,1)}), bf16[256,8,128]{2,0,1:T(8,128)(2,1)S(1)}, u32[]{:S(2)}, u32[]{:S(2)}) async-start(bf16[256,8,128]{2,0,1:T(8,128)(2,1)} %copy_bitcast_fusion.1), calls=%async_computation.2 | async-start | bytes 1048576 | tf_op jit(solution)/shard_map/all_to_all | solution.py:149
  27.3 134.0 %all-reduce.5.cloned.1.call-start = ((), (), s32[]{:S(2)}) async-start(), calls=%async_computation.5 | async-start | bytes 131072 | tf_op jit(solution)/shard_map/psum | solution.py:172
  27.8 1.3 copy-start.1
  27.9 135.7 %copy-start.7 = (bf16[512]{0:T(512)(128)(2,1)S(1)}, bf16[512]{0:T(512)(128)(2,1)}, u32[]{:S(2)}) copy-start(bf16[512]{0:T(512)(128)(2,1)} %param.26) | copy-start | bytes 3076
  27.9 205.9 %copy-start.5 = (bf16[32,512]{1,0:T(8,128)(2,1)S(1)}, bf16[32,512]{1,0:T(8,128)(2,1)}, u32[]{:S(2)}) copy-start(bf16[32,512]{1,0:T(8,128)(2,1)} %param.24) | copy-start | bytes 98308
  36.4 197.4 %all-reduce.7.cloned.1.call-start = ((), (), s32[]{:S(2)}) async-start(), calls=%async_computation.6 | async-start | bytes 131072 | tf_op jit(solution)/shard_map/psum | solution.py:174
  163.5 247.8 %all-reduce.9.cloned.1.call-start = ((), (), s32[]{:S(2)}) async-start(), calls=%async_computation.8 | async-start | bytes 1048576 | tf_op jit(solution)/shard_map/psum | solution.py:182
  268.1 147.2 %copy-start.3 = (bf16[256,1024]{1,0:T(8,128)(2,1)S(1)}, bf16[256,1024]{1,0:T(8,128)(2,1)}, u32[]{:S(2)}) copy-start(bf16[256,1024]{1,0:T(8,128)(2,1)} %param.20) | copy-start | bytes 1572868
  272.2 210.6 %reduce-scatter.4.cloned.1.call-start = ((), (), s32[]{:S(2)}) async-start(), calls=%async_computation.7 | async-start | bytes 294912
  414.7 170.4 %all-gather.2.cloned.1.call-start = ((), (), s32[]{:S(2)}) async-start(), calls=%async_computation.4 | async-start | bytes 4718592 | tf_op jit(solution)/shard_map/all_gather | solution.py:156
  417.9 66.4 %all-to-all-start = ((bf16[8,256,1024]{2,1,0:T(8,128)(2,1)}), bf16[8,256,1024]{2,1,0:T(8,128)(2,1)}, u32[]{:S(2)}, u32[]{:S(2)}) async-start(bf16[8,256,1024]{2,1,0:T(8,128)(2,1)} %stack.2), calls=%async_computation | async-start | bytes 8388608 | tf_op jit(solution)/shard_map/all_to_all | solution.py:158
  585.2 163.5 %copy-start.6 = (pred[256]{0:T(512)(128)(4,1)S(1)}, pred[256]{0:T(512)(128)(4,1)}, u32[]{:S(2)}) copy-start(pred[256]{0:T(512)(128)(4,1)} %get-tuple-element.31) | copy-start | bytes 772
  585.9 5.4 copy-start.2
Sparse Core Ops, SparseCore 0:
  36.5 124.7 all-reduce.4
  164.5 69.2 all-reduce.6
  272.3 138.9 all-reduce.8
  414.9 67.8 reduce-scatter.3
  484.3 100.8 all-gather.1
